TPU v7x, 32 devices: a whole 2x2x4 slice. The times are simulated.
32 devices in a mesh: dp: 16 (over z, x, core), mp: 2 (over y).
Axes of the slice: x: 2, y: 2, z: 4, core: 2. Of those that a mesh axis runs over, the one named last changes fastest.
Arguments:
- tokens: bfloat16 [64, 512, 768], P('dp', 'mp'), may hold values from -6 to 6
- lengths: int32 [64], P('dp'), may hold values from 128 to 512, as said below
- out_grad: bfloat16 [64, 512, 768], P('dp', 'mp'), may hold values from -6 to 6
- ln1_gain: float32 [768], replicated, may hold values from 0.25 to 1.75
- ln1_shift: float32 [768], replicated, may hold values from -1.75 to 1.75
- w_query: bfloat16 [768, 768], P(None, 'mp'), may hold values from -0.21875 to 0.21875
- b_query: float32 [768], P('mp'), may hold values from -3 to 3
- w_key: bfloat16 [768, 768], P(None, 'mp'), may hold values from -0.21875 to 0.21875
- w_value: bfloat16 [768, 768], P(None, 'mp'), may hold values from -0.21875 to 0.21875
- b_value: float32 [768], P('mp'), may hold values from -3 to 3
- w_out: bfloat16 [768, 768], P('mp'), may hold values from -1.75 to 1.75
- b_out: float32 [768], replicated, may hold values from -1.75 to 1.75
- ln2_gain: float32 [768], replicated, may hold values from 0.25 to 1.75
- ln2_shift: float32 [768], replicated, may hold values from -1.75 to 1.75
- w_up: bfloat16 [768, 3072], P(None, 'mp'), may hold values from -0.21875 to 0.21875
- b_up: float32 [3072], P('mp'), may hold values from -3 to 3
- w_down: bfloat16 [3072, 768], P('mp'), may hold values from -0.109375 to 0.109375
- b_down: float32 [768], replicated, may hold values from -1.75 to 1.75
Outputs:
- block_out: bfloat16 [64, 512, 768], P('dp', 'mp')
- input_grad: float32 [64, 512, 768], P('dp', 'mp')
- grad_ln1_gain: float32 [768], replicated
- grad_ln1_shift: float32 [768], replicated
- grad_w_query: float32 [768, 768], P(None, 'mp')
- grad_b_query: float32 [768], P('mp')
- grad_w_key: float32 [768, 768], P(None, 'mp')
- grad_w_value: float32 [768, 768], P(None, 'mp')
- grad_b_value: float32 [768], P('mp')
- grad_w_out: float32 [768, 768], P('mp')
- grad_b_out: float32 [768], replicated
- grad_ln2_gain: float32 [768], replicated
- grad_ln2_shift: float32 [768], replicated
- grad_w_up: float32 [768, 3072], P(None, 'mp')
- grad_b_up: float32 [3072], P('mp')
- grad_w_down: float32 [3072, 768], P('mp')
- grad_b_down: float32 [768], replicated
Inputs may be any that keep to these rules, and one draw needn't show every extreme that they name: lengths of the rows; some row has 512 and some row a quarter of 512.
All inputs are finite; a program needn't handle non-finite values.
Results may differ from a plain program's by a relative error of at most 0.013.
The roundings to bfloat16 on the way count: a program that leaves them out, or rounds other values in their place, can miss the bound.
Values may be sent and summed in bfloat16 or wider, within the bound.
No kernel may reach another device: no remote copies, remote signals or barrier semaphores. Data moves between devices by JAX's collectives and lax.ppermute only.
A program may use at most 192 MiB of HBM per device.

v0:
```python
import math
import jax
import jax.numpy as jnp
from jax import lax
from jax.sharding import PartitionSpec as P

HEAD_DIM = 64
SEQ = 512
MB = 4
ROWS_MB = 1
epsilon = 1e-12
masked_fill = -1000000000.0


def layer_norm(values, gain_vec, offset):
    average = jnp.mean(values, axis=-1, keepdims=True)
    centred = values - average
    inv_std = lax.rsqrt(jnp.mean(centred * centred, axis=-1, keepdims=True) + epsilon)
    unit_part = centred * inv_std
    return (unit_part * gain_vec + offset, unit_part, inv_std)


def norm_back(upstream, unit_part, inv_std, gain_vec):
    scaled = upstream * gain_vec
    return inv_std * (
        scaled
        - jnp.mean(scaled, axis=-1, keepdims=True)
        - unit_part * jnp.mean(scaled * unit_part, axis=-1, keepdims=True)
    )


def gelu_slope(values):
    normal_cdf = 0.5 * (1.0 + lax.erf(values * (1.0 / math.sqrt(2.0))))
    return normal_cdf + values * jnp.exp(-0.5 * values * values) * (1.0 / math.sqrt(2.0 * math.pi))


def product(pattern, left_side, right_side):
    return jnp.einsum(pattern, left_side, right_side, preferred_element_type=jnp.float32)


def token_sum(values):
    return jnp.sum(values, axis=(0, 1))


def masked_scores(query_low, keys_low, key_valid, score_scale):
    raw_scores = product("bqhd,bkhd->bhqk", query_low, keys_low) * score_scale
    return jnp.where(key_valid, raw_scores, masked_fill)


def on_device(
    tokens,
    lengths,
    out_grad,
    ln1_gain,
    ln1_shift,
    w_query,
    b_query,
    w_key,
    w_value,
    b_value,
    w_out,
    b_out,
    ln2_gain,
    ln2_shift,
    w_up,
    b_up,
    w_down,
    b_down,
):
    heads_here = w_query.shape[1] // HEAD_DIM
    score_scale = 1.0 / math.sqrt(HEAD_DIM)
    positions = jnp.arange(SEQ, dtype=jnp.int32)
    sum_w_query = jnp.zeros(w_query.shape, jnp.float32)
    sum_b_query = jnp.zeros(b_query.shape, jnp.float32)
    sum_w_key = jnp.zeros(w_key.shape, jnp.float32)
    sum_w_value = jnp.zeros(w_value.shape, jnp.float32)
    sum_b_value = jnp.zeros(b_value.shape, jnp.float32)
    sum_w_out = jnp.zeros(w_out.shape, jnp.float32)
    sum_w_up = jnp.zeros(w_up.shape, jnp.float32)
    sum_b_up = jnp.zeros(b_up.shape, jnp.float32)
    sum_w_down = jnp.zeros(w_down.shape, jnp.float32)
    sum_ln1_gain = jnp.zeros(ln1_gain.shape, jnp.float32)
    sum_ln1_shift = jnp.zeros(ln1_shift.shape, jnp.float32)
    sum_ln2_gain = jnp.zeros(ln2_gain.shape, jnp.float32)
    sum_ln2_shift = jnp.zeros(ln2_shift.shape, jnp.float32)
    sum_b_out = jnp.zeros(b_out.shape, jnp.float32)
    sum_b_down = jnp.zeros(b_down.shape, jnp.float32)
    outputs = []
    input_grads = []
    for micro_idx in range(MB):
        row_start = micro_idx * ROWS_MB
        inputs = tokens[row_start : row_start + ROWS_MB].astype(jnp.float32)
        row_lengths = lengths[row_start : row_start + ROWS_MB]
        upstream = out_grad[row_start : row_start + ROWS_MB]
        normed_in, unit_in, inv_in = layer_norm(inputs, ln1_gain, ln1_shift)
        full_in = lax.all_gather(normed_in.astype(jnp.bfloat16), "mp", axis=1, tiled=True)
        rows_mb = full_in.shape[0]
        query_low = (
            (product("bsd,de->bse", full_in, w_query) + b_query)
            .astype(jnp.bfloat16)
            .reshape(rows_mb, SEQ, heads_here, HEAD_DIM)
        )
        keys_low = (
            product("bsd,de->bse", full_in, w_key)
            .astype(jnp.bfloat16)
            .reshape(rows_mb, SEQ, heads_here, HEAD_DIM)
        )
        values_low = (
            (product("bsd,de->bse", full_in, w_value) + b_value)
            .astype(jnp.bfloat16)
            .reshape(rows_mb, SEQ, heads_here, HEAD_DIM)
        )
        key_valid = (positions[None, :] < row_lengths[:, None])[:, None, None, :]
        scores = masked_scores(query_low, keys_low, key_valid, score_scale)
        row_max = jnp.max(scores, axis=-1, keepdims=True)
        log_total = row_max + jnp.log(jnp.sum(jnp.exp(scores - row_max), axis=-1, keepdims=True))
        prob_low = jnp.exp(scores - log_total).astype(jnp.bfloat16)
        mixed_low = (
            product("bhqk,bkhd->bqhd", prob_low, values_low)
            .reshape(rows_mb, SEQ, heads_here * HEAD_DIM)
            .astype(jnp.bfloat16)
        )
        attended = lax.psum_scatter(
            product("bse,ed->bsd", mixed_low, w_out), "mp", scatter_dimension=1, tiled=True
        )
        residual = inputs + attended + b_out
        normed_mid, unit_mid, inv_mid = layer_norm(residual, ln2_gain, ln2_shift)
        full_mid = lax.all_gather(normed_mid.astype(jnp.bfloat16), "mp", axis=1, tiled=True)
        hidden = product("bsd,df->bsf", full_mid, w_up) + b_up
        active = jax.nn.gelu(hidden, approximate=False).astype(jnp.bfloat16)
        branch = lax.psum_scatter(
            product("bsf,fd->bsd", active, w_down).astype(jnp.bfloat16),
            "mp",
            scatter_dimension=1,
            tiled=True,
        ).astype(jnp.float32)
        outputs.append((residual + branch + b_down).astype(jnp.bfloat16))
        grad_full = lax.all_gather(upstream, "mp", axis=1, tiled=True)
        upstream_f = upstream.astype(jnp.float32)
        sum_w_down = sum_w_down + product("bsf,bsd->fd", active, grad_full)
        sum_b_down = sum_b_down + token_sum(upstream_f)
        grad_hidden = (product("bsd,fd->bsf", grad_full, w_down) * gelu_slope(hidden)).astype(
            jnp.bfloat16
        )
        sum_w_up = sum_w_up + product("bsd,bsf->df", full_mid, grad_hidden)
        sum_b_up = sum_b_up + token_sum(grad_hidden.astype(jnp.float32))
        grad_norm_mid = lax.psum_scatter(
            product("bsf,df->bsd", grad_hidden, w_up), "mp", scatter_dimension=1, tiled=True
        )
        sum_ln2_gain = sum_ln2_gain + token_sum(grad_norm_mid * unit_mid)
        sum_ln2_shift = sum_ln2_shift + token_sum(grad_norm_mid)
        grad_residual = upstream_f + norm_back(grad_norm_mid, unit_mid, inv_mid, ln2_gain)
        sum_b_out = sum_b_out + token_sum(grad_residual)
        grad_attn = lax.all_gather(grad_residual.astype(jnp.bfloat16), "mp", axis=1, tiled=True)
        sum_w_out = sum_w_out + product("bse,bsd->ed", mixed_low, grad_attn)
        grad_mixed = (
            product("bsd,ed->bse", grad_attn, w_out)
            .astype(jnp.bfloat16)
            .reshape(rows_mb, SEQ, heads_here, HEAD_DIM)
        )
        grad_probs = product("bqhd,bkhd->bhqk", grad_mixed, values_low)
        probs_full = jnp.exp(masked_scores(query_low, keys_low, key_valid, score_scale) - log_total)
        row_delta = jnp.sum(probs_full * grad_probs, axis=-1, keepdims=True)
        grad_scores = (probs_full * (grad_probs - row_delta)).astype(jnp.bfloat16)
        grad_query = (
            (product("bhqk,bkhd->bqhd", grad_scores, keys_low) * score_scale)
            .astype(jnp.bfloat16)
            .reshape(rows_mb, SEQ, heads_here * HEAD_DIM)
        )
        grad_keys = (
            (product("bhqk,bqhd->bkhd", grad_scores, query_low) * score_scale)
            .astype(jnp.bfloat16)
            .reshape(rows_mb, SEQ, heads_here * HEAD_DIM)
        )
        grad_values = (
            product("bhqk,bqhd->bkhd", prob_low, grad_mixed)
            .astype(jnp.bfloat16)
            .reshape(rows_mb, SEQ, heads_here * HEAD_DIM)
        )
        sum_w_query = sum_w_query + product("bsd,bse->de", full_in, grad_query)
        sum_b_query = sum_b_query + token_sum(grad_query.astype(jnp.float32))
        sum_w_key = sum_w_key + product("bsd,bse->de", full_in, grad_keys)
        sum_w_value = sum_w_value + product("bsd,bse->de", full_in, grad_values)
        sum_b_value = sum_b_value + token_sum(grad_values.astype(jnp.float32))
        input_terms = (
            product("bse,de->bsd", grad_query, w_query)
            + product("bse,de->bsd", grad_keys, w_key)
            + product("bse,de->bsd", grad_values, w_value)
        )
        grad_norm_in = lax.psum_scatter(
            input_terms.astype(jnp.bfloat16), "mp", scatter_dimension=1, tiled=True
        ).astype(jnp.float32)
        sum_ln1_gain = sum_ln1_gain + token_sum(grad_norm_in * unit_in)
        sum_ln1_shift = sum_ln1_shift + token_sum(grad_norm_in)
        input_grads.append(grad_residual + norm_back(grad_norm_in, unit_in, inv_in, ln1_gain))
    totals = tuple(
        lax.psum(
            (
                sum_w_query,
                sum_b_query,
                sum_w_key,
                sum_w_value,
                sum_b_value,
                sum_w_out,
                sum_w_up,
                sum_b_up,
                sum_w_down,
            ),
            "dp",
        )
    )
    common = lax.psum(
        (sum_ln1_gain, sum_ln1_shift, sum_ln2_gain, sum_ln2_shift, sum_b_out, sum_b_down),
        ("dp", "mp"),
    )
    block_out = jnp.concatenate(outputs, axis=0)
    input_grad = jnp.concatenate(input_grads, axis=0)
    return (
        block_out,
        input_grad,
        common[0],
        common[1],
        totals[0],
        totals[1],
        totals[2],
        totals[3],
        totals[4],
        totals[5],
        common[4],
        common[2],
        common[3],
        totals[6],
        totals[7],
        totals[8],
        common[5],
    )


def solution(mesh):
    in_specs = (
        P("dp", "mp", None),
        P("dp"),
        P("dp", "mp", None),
        P(),
        P(),
        P(None, "mp"),
        P("mp"),
        P(None, "mp"),
        P(None, "mp"),
        P("mp"),
        P("mp", None),
        P(),
        P(),
        P(),
        P(None, "mp"),
        P("mp"),
        P("mp", None),
        P(),
    )
    out_specs = (
        P("dp", "mp", None),
        P("dp", "mp", None),
        P(),
        P(),
        P(None, "mp"),
        P("mp"),
        P(None, "mp"),
        P(None, "mp"),
        P("mp"),
        P("mp", None),
        P(),
        P(),
        P(),
        P(None, "mp"),
        P("mp"),
        P("mp", None),
        P(),
    )
    return jax.shard_map(
        on_device, mesh=mesh, in_specs=in_specs, out_specs=out_specs, check_vma=False
    )
```

profile of v0, /device:TPU:0, one launch (start us, length us, event | category | flops | bytes accessed | tf_op | source)
XLA Modules:
  0.0 932.4 jit_solution(8912068039627414131)
XLA Ops:
  12.2 12.8 %all_gather.52 = bf16[1,512,768]{2,1,0:T(8,128)(2,1)S(1)} all-gather(bf16[1,256,768]{2,1,0:T(8,128)(2,1)S(1)} %fusion.127), channel_id=1, replica_groups=mesh['dp'=16,'mp'=2] {'mp'}, dimensions={1}, use_global_device_ids=true | all-gather | bytes 1179648 | tf_op jit(solution)/shard_map/all_gather | solution.py:96
  40.5 16.8 %all_gather.60 = bf16[1,512,768]{2,1,0:T(8,128)(2,1)} all-gather(bf16[1,256,768]{2,1,0:T(8,128)(2,1)S(1)} %get-tuple-element.113), channel_id=1, replica_groups=mesh['dp'=16,'mp'=2] {'mp'}, dimensions={1}, use_global_device_ids=true | all-gather | bytes 1179648 | tf_op jit(solution)/shard_map/all_gather | solution.py:138
  57.3 12.3 %reduce-scatter.25.cloned.1.call-done = f32[1,256,768]{2,1,0:T(8,128)} async-done(((f32[1,512,768]{2,1,0:T(8,128)}), f32[1,256,768]{2,1,0:T(8,128)}) %reduce-scatter.25.cloned.1.call-update) | async-done | bytes 786448 | tf_op jit(solution)/shard_map/reduce_scatter | solution.py:123
  72.2 12.0 %all_gather.53 = bf16[1,512,768]{2,1,0:T(8,128)(2,1)S(1)} all-gather(bf16[1,256,768]{2,1,0:T(8,128)(2,1)S(1)} %add_convert_fusion.7), channel_id=1, replica_groups=mesh['dp'=16,'mp'=2] {'mp'}, dimensions={1}, use_global_device_ids=true | all-gather | bytes 1179648 | tf_op jit(solution)/shard_map/all_gather | solution.py:128
  84.2 10.3 %fusion.16 = (bf16[512,1536]{1,0:T(8,128)(2,1)}, f32[512,1536]{1,0:T(8,128)S(1)}) fusion(f32[1536]{0:T(1024)} %param.33, bf16[768,1536]{1,0:T(8,128)(2,1)S(1)} %copy-done, bf16[1,512,768]{2,1,0:T(8,128)(2,1)S(1)} %all_gather.53), kind=kOutput, calls=%fused_computation.54 | convolution fusion | flops 1259864064 | bytes 7870464 | tf_op jit(solution)/shard_map/bsd,df->bsf/dot_general | solution.py:38
  105.7 22.8 %reduce-scatter.41.cloned.1.call-done = f32[1,256,768]{2,1,0:T(8,128)} async-done(((f32[1,512,768]{2,1,0:T(8,128)}), f32[1,256,768]{2,1,0:T(8,128)}) %reduce-scatter.41.cloned.1.call-update) | async-done | bytes 786448 | tf_op jit(solution)/shard_map/reduce_scatter | solution.py:147
  131.2 17.6 %reduce-scatter.27.cloned.1.call-done = bf16[1,256,768]{2,1,0:T(8,128)(2,1)} async-done(((bf16[1,512,768]{2,1,0:T(8,128)(2,1)}), bf16[1,256,768]{2,1,0:T(8,128)(2,1)}) %reduce-scatter.27.cloned.1.call-update) | async-done | bytes 393232 | tf_op jit(solution)/shard_map/reduce_scatter | solution.py:131
  152.5 12.1 %all_gather.61 = bf16[1,512,768]{2,1,0:T(8,128)(2,1)S(1)} all-gather(bf16[1,256,768]{2,1,0:T(8,128)(2,1)S(1)} %convert_element_type.620), channel_id=1, replica_groups=mesh['dp'=16,'mp'=2] {'mp'}, dimensions={1}, use_global_device_ids=true | all-gather | bytes 1179648 | tf_op jit(solution)/shard_map/all_gather | solution.py:154
  181.2 15.7 %reduce-scatter.43.cloned.1.call-done = bf16[1,256,768]{2,1,0:T(8,128)(2,1)} async-done(((bf16[1,512,768]{2,1,0:T(8,128)(2,1)}), bf16[1,256,768]{2,1,0:T(8,128)(2,1)}) %reduce-scatter.43.cloned.1.call-update) | async-done | bytes 393232 | tf_op jit(solution)/shard_map/reduce_scatter | solution.py:190
  202.5 11.8 %all_gather.54 = bf16[1,512,768]{2,1,0:T(8,128)(2,1)S(1)} all-gather(bf16[1,256,768]{2,1,0:T(8,128)(2,1)S(1)} %get-tuple-element.97), channel_id=1, replica_groups=mesh['dp'=16,'mp'=2] {'mp'}, dimensions={1}, use_global_device_ids=true | all-gather | bytes 1179648 | tf_op jit(solution)/shard_map/all_gather | solution.py:96
  228.0 16.7 %all_gather.50 = bf16[1,512,768]{2,1,0:T(8,128)(2,1)S(1)} all-gather(bf16[1,256,768]{2,1,0:T(8,128)(2,1)} %get-tuple-element.96), channel_id=1, replica_groups=mesh['dp'=16,'mp'=2] {'mp'}, dimensions={1}, use_global_device_ids=true | all-gather | bytes 1179648 | tf_op jit(solution)/shard_map/all_gather | solution.py:96
  259.6 9.8 %all_gather.48 = bf16[1,512,768]{2,1,0:T(8,128)(2,1)S(1)} all-gather(bf16[1,256,768]{2,1,0:T(8,128)(2,1)} %get-tuple-element.95), channel_id=1, replica_groups=mesh['dp'=16,'mp'=2] {'mp'}, dimensions={1}, use_global_device_ids=true | all-gather | bytes 1179648 | tf_op jit(solution)/shard_map/all_gather | solution.py:96
  283.6 10.3 %all_gather.62 = bf16[1,512,768]{2,1,0:T(8,128)(2,1)} all-gather(bf16[1,256,768]{2,1,0:T(8,128)(2,1)} %get-tuple-element.112), channel_id=1, replica_groups=mesh['dp'=16,'mp'=2] {'mp'}, dimensions={1}, use_global_device_ids=true | all-gather | bytes 1179648 | tf_op jit(solution)/shard_map/all_gather | solution.py:138
  293.9 17.9 %all_gather.58 = bf16[1,512,768]{2,1,0:T(8,128)(2,1)} all-gather(bf16[1,256,768]{2,1,0:T(8,128)(2,1)} %get-tuple-element.111), channel_id=1, replica_groups=mesh['dp'=16,'mp'=2] {'mp'}, dimensions={1}, use_global_device_ids=true | all-gather | bytes 1179648 | tf_op jit(solution)/shard_map/all_gather | solution.py:138
  311.8 16.6 %all_gather.56 = bf16[1,512,768]{2,1,0:T(8,128)(2,1)} all-gather(bf16[1,256,768]{2,1,0:T(8,128)(2,1)S(1)} %copy-done.115), channel_id=1, replica_groups=mesh['dp'=16,'mp'=2] {'mp'}, dimensions={1}, use_global_device_ids=true | all-gather | bytes 1179648 | tf_op jit(solution)/shard_map/all_gather | solution.py:138
  332.8 11.8 %all_gather.55 = bf16[1,512,768]{2,1,0:T(8,128)(2,1)} all-gather(bf16[1,256,768]{2,1,0:T(8,128)(2,1)S(1)} %get-tuple-element.120), channel_id=1, replica_groups=mesh['dp'=16,'mp'=2] {'mp'}, dimensions={1}, use_global_device_ids=true | all-gather | bytes 1179648 | tf_op jit(solution)/shard_map/all_gather | solution.py:128
  344.7 10.9 %all_gather.51 = bf16[1,512,768]{2,1,0:T(8,128)(2,1)S(1)} all-gather(bf16[1,256,768]{2,1,0:T(8,128)(2,1)S(1)} %get-tuple-element.119), channel_id=1, replica_groups=mesh['dp'=16,'mp'=2] {'mp'}, dimensions={1}, use_global_device_ids=true | all-gather | bytes 1179648 | tf_op jit(solution)/shard_map/all_gather | solution.py:128
  355.6 9.4 %fusion.13 = (bf16[512,1536]{1,0:T(8,128)(2,1)}, f32[512,1536]{1,0:T(8,128)S(1)}) fusion(f32[1536]{0:T(1024)S(1)} %copy-done.189, bf16[768,1536]{1,0:T(8,128)(2,1)S(1)} %copy-done, bf16[1,512,768]{2,1,0:T(8,128)(2,1)S(1)} %all_gather.51), kind=kOutput, calls=%fused_computation.51 | convolution fusion | flops 1259864064 | bytes 7870464 | tf_op jit(solution)/shard_map/bsd,df->bsf/dot_general | solution.py:38
  365.0 10.5 %all_gather.49 = bf16[1,512,768]{2,1,0:T(8,128)(2,1)} all-gather(bf16[1,256,768]{2,1,0:T(8,128)(2,1)S(1)} %get-tuple-element.118), channel_id=1, replica_groups=mesh['dp'=16,'mp'=2] {'mp'}, dimensions={1}, use_global_device_ids=true | all-gather | bytes 1179648 | tf_op jit(solution)/shard_map/all_gather | solution.py:128
  382.2 9.8 %fusion.19 = (bf16[512,1536]{1,0:T(8,128)(2,1)}, f32[512,1536]{1,0:T(8,128)S(1)}) fusion(f32[1536]{0:T(1024)S(1)} %copy-done.189, bf16[768,1536]{1,0:T(8,128)(2,1)S(1)} %copy-done, bf16[1,512,768]{2,1,0:T(8,128)(2,1)} %all_gather.55), kind=kOutput, calls=%fused_computation.57 | convolution fusion | flops 1259864064 | bytes 7870464 | tf_op jit(solution)/shard_map/bsd,df->bsf/dot_general | solution.py:38
  398.9 9.8 %fusion.10 = (bf16[512,1536]{1,0:T(8,128)(2,1)}, f32[512,1536]{1,0:T(8,128)S(1)}) fusion(f32[1536]{0:T(1024)S(1)} %copy-done.189, bf16[768,1536]{1,0:T(8,128)(2,1)S(1)} %copy-done, bf16[1,512,768]{2,1,0:T(8,128)(2,1)} %all_gather.49), kind=kOutput, calls=%fused_computation.48 | convolution fusion | flops 1259864064 | bytes 7870464 | tf_op jit(solution)/shard_map/bsd,df->bsf/dot_general | solution.py:38
  420.0 5.4 fusion.162
  450.2 9.8 %add_add_fusion = f32[1536,768]{1,0:T(8,128)} fusion(f32[1536,768]{1,0:T(8,128)} %fusion.162, f32[1536,768]{1,0:T(8,128)} %fusion.173, f32[1536,768]{1,0:T(8,128)} %fusion.167, bf16[512,1536]{1,0:T(8,128)(2,1)} %get-tuple-element.145, bf16[1,512,768]{2,1,0:T(8,128)(2,1)} %all_gather.62), kind=kOutput, calls=%fused_computation.32 | convolution fusion | flops 1211498496 | bytes 21233664 | tf_op jit(solution)/shard_map/bsf,bsd->fd/dot_general | solution.py:38
  460.0 9.1 add_add_fusion.1
  472.8 13.2 %reduce-scatter.19.cloned.1.call-done = bf16[1,256,768]{2,1,0:T(8,128)(2,1)} async-done(((bf16[1,512,768]{2,1,0:T(8,128)(2,1)}), bf16[1,256,768]{2,1,0:T(8,128)(2,1)}) %reduce-scatter.19.cloned.1.call-update) | async-done | bytes 393232 | tf_op jit(solution)/shard_map/reduce_scatter | solution.py:131
  486.1 20.2 %reduce-scatter.31.cloned.1.call-done = bf16[1,256,768]{2,1,0:T(8,128)(2,1)} async-done(((bf16[1,512,768]{2,1,0:T(8,128)(2,1)}), bf16[1,256,768]{2,1,0:T(8,128)(2,1)}) %reduce-scatter.31.cloned.1.call-update) | async-done | bytes 393232 | tf_op jit(solution)/shard_map/reduce_scatter | solution.py:131
  511.3 19.5 %all_gather.57 = bf16[1,512,768]{2,1,0:T(8,128)(2,1)S(1)} all-gather(bf16[1,256,768]{2,1,0:T(8,128)(2,1)S(1)} %convert_element_type.586), channel_id=1, replica_groups=mesh['dp'=16,'mp'=2] {'mp'}, dimensions={1}, use_global_device_ids=true | all-gather | bytes 1179648 | tf_op jit(solution)/shard_map/all_gather | solution.py:154
  547.8 8.5 all_gather.59
  568.1 8.6 all_gather.63
  642.5 60.4 %all-reduce.1 = (f32[384]{0:T(512)}, f32[384]{0:T(512)}, f32[1536]{0:T(1024)}) all-reduce(f32[384]{0:T(512)} %add.700, f32[384]{0:T(512)} %add.710, f32[1536]{0:T(1024)S(1)} %add_add_fusion.2), channel_id=1, replica_groups=mesh['dp'=16,'mp'=2] {'dp'}, use_global_device_ids=true, to_apply=%region_75.76 | all-reduce | flops 2304 | bytes 18432 | tf_op jit(solution)/shard_map/psum | solution.py:197
  713.4 39.4 %all-reduce = (f32[768]{0:T(1024)}, f32[768]{0:T(1024)}, f32[768]{0:T(1024)}, f32[768]{0:T(1024)}, f32[768]{0:T(1024)}, /*index=5*/f32[768]{0:T(1024)}) all-reduce(f32[768]{0:T(1024)} %add_add_fusion.10, f32[768]{0:T(1024)} %add_add_fusion.9, f32[768]{0:T(1024)} %add_add_fusion.6, ...), channel_id=1, replica_groups=mesh['dp'=16,'mp'=2] {'dp','mp'}, use_global_device_ids=true, to_apply=%region_64.65 | all-reduce | flops 4608 | bytes 36864 | tf_op jit(solution)/shard_map/psum | solution.py:212
  763.1 151.8 %all-reduce.5.cloned.1.call-done = (f32[768,384]{1,0:T(8,128)}, f32[768,384]{1,0:T(8,128)}, f32[768,384]{1,0:T(8,128)}, f32[384,768]{1,0:T(8,128)}, f32[768,1536]{1,0:T(8,128)}, /*index=5*/f32[1536,768]{1,0:T(8,128)}) async-done(((f32[768,384]{1,0:T(8,128)}, f32[768,384]{1,0:T(8,128)}, f32[768,384]{1,0:T(8,128)}, f32[384,768]{1,0:T(8,128)}, f32[768,1536]{1,0:T(8,128)}, /*index=5*/f32[1536,768]{1,0:T(8,128)}), ...) | async-done | bytes 14155792 | tf_op jit(solution)/shard_map/psum | solution.py:197
  (646 shorter events, 292.1 us)
Async XLA Ops:
  7.2 77.0 %copy-start = (bf16[768,1536]{1,0:T(8,128)(2,1)S(1)}, bf16[768,1536]{1,0:T(8,128)(2,1)}, u32[]{:S(2)}) copy-start(bf16[768,1536]{1,0:T(8,128)(2,1)} %param.32) | copy-start | bytes 7077892
  7.2 62.3 %reduce-scatter.25.cloned.1.call-start = ((), (), s32[]{:S(2)}) async-start(), calls=%async_computation.20 | async-start | bytes 2359296 | tf_op jit(solution)/shard_map/reduce_scatter | solution.py:123
  38.0 90.5 %reduce-scatter.41.cloned.1.call-start = ((), (), s32[]{:S(2)}) async-start(), calls=%async_computation.28 | async-start | bytes 2359296 | tf_op jit(solution)/shard_map/reduce_scatter | solution.py:147
  101.1 47.7 %reduce-scatter.27.cloned.1.call-start = ((), (), s32[]{:S(2)}) async-start(), calls=%async_computation.21 | async-start | bytes 1179648 | tf_op jit(solution)/shard_map/reduce_scatter | solution.py:131
  105.6 91.3 %reduce-scatter.43.cloned.1.call-start = ((), (), s32[]{:S(2)}) async-start(), calls=%async_computation.29 | async-start | bytes 1179648 | tf_op jit(solution)/shard_map/reduce_scatter | solution.py:190
  179.3 149.1 %reduce-scatter.29.cloned.1.call-start = ((), (), s32[]{:S(2)}) async-start(), calls=%async_computation.22 | async-start | bytes 2359296 | tf_op jit(solution)/shard_map/reduce_scatter | solution.py:123
  180.5 35.0 %copy-start.144 = (f32[256]{0:T(256)}, f32[256]{0:T(256)S(1)}, u32[]{:S(2)}) copy-start(f32[256]{0:T(256)S(1)} %broadcast_multiply_fusion.17) | copy-start | bytes 3076
  181.2 34.4 %copy-start.148 = (f32[256]{0:T(256)}, f32[256]{0:T(256)S(1)}, u32[]{:S(2)}) copy-start(f32[256]{0:T(256)S(1)} %get-tuple-element.182) | copy-start | bytes 3076
  227.3 101.2 %reduce-scatter.21.cloned.1.call-start = ((), (), s32[]{:S(2)}) async-start(), calls=%async_computation.18 | async-start | bytes 2359296 | tf_op jit(solution)/shard_map/reduce_scatter | solution.py:123
  258.8 70.4 %reduce-scatter.17.cloned.1.call-start = ((), (), s32[]{:S(2)}) async-start(), calls=%async_computation.16 | async-start | bytes 2359296 | tf_op jit(solution)/shard_map/reduce_scatter | solution.py:123
  283.5 45.7 %copy-start.166 = (f32[768]{0:T(1024)S(1)}, f32[768]{0:T(1024)}, u32[]{:S(2)}) copy-start(f32[768]{0:T(1024)} %param.29) | copy-start | bytes 9220
  283.5 185.6 %reduce-scatter.37.cloned.1.call-start = ((), (), s32[]{:S(2)}) async-start(), calls=%async_computation.26 | async-start | bytes 2359296 | tf_op jit(solution)/shard_map/reduce_scatter | solution.py:147
  331.8 137.2 %copy-start.146 = (f32[256]{0:T(256)}, f32[256]{0:T(256)S(1)}, u32[]{:S(2)}) copy-start(f32[256]{0:T(256)S(1)} %broadcast_multiply_fusion.20) | copy-start | bytes 3076
  332.1 137.0 %copy-start.172 = (f32[256]{0:T(256)}, f32[256]{0:T(256)S(1)}, u32[]{:S(2)}) copy-start(f32[256]{0:T(256)S(1)} %add_rsqrt_fusion.4) | copy-start | bytes 3076
  382.1 87.0 %reduce-scatter.45.cloned.1.call-start = ((), (), s32[]{:S(2)}) async-start(), calls=%async_computation.30 | async-start | bytes 2359296 | tf_op jit(solution)/shard_map/reduce_scatter | solution.py:147
  398.6 70.4 %reduce-scatter.33.cloned.1.call-start = ((), (), s32[]{:S(2)}) async-start(), calls=%async_computation.24 | async-start | bytes 2359296 | tf_op jit(solution)/shard_map/reduce_scatter | solution.py:147
  415.3 70.8 %reduce-scatter.19.cloned.1.call-start = ((), (), s32[]{:S(2)}) async-start(), calls=%async_computation.17 | async-start | bytes 1179648 | tf_op jit(solution)/shard_map/reduce_scatter | solution.py:131
  419.9 86.4 %reduce-scatter.31.cloned.1.call-start = ((), (), s32[]{:S(2)}) async-start(), calls=%async_computation.23 | async-start | bytes 1179648 | tf_op jit(solution)/shard_map/reduce_scatter | solution.py:131
  434.9 109.7 %reduce-scatter.23.cloned.1.call-start = ((), (), s32[]{:S(2)}) async-start(), calls=%async_computation.19 | async-start | bytes 1179648 | tf_op jit(solution)/shard_map/reduce_scatter | solution.py:131
  450.2 257.0 %reduce-scatter.35.cloned.1.call-start = ((), (), s32[]{:S(2)}) async-start(), calls=%async_computation.25 | async-start | bytes 1179648 | tf_op jit(solution)/shard_map/reduce_scatter | solution.py:190
  469.1 37.2 %copy-start.142 = (f32[768]{0:T(1024)S(1)}, f32[768]{0:T(1024)}, u32[]{:S(2)}) copy-start(f32[768]{0:T(1024)} %param.35) | copy-start | bytes 9220
  588.7 118.5 %reduce-scatter.39.cloned.1.call-start = ((), (), s32[]{:S(2)}) async-start(), calls=%async_computation.27 | async-start | bytes 1179648 | tf_op jit(solution)/shard_map/reduce_scatter | solution.py:190
  609.2 98.0 %reduce-scatter.47.cloned.1.call-start = ((), (), s32[]{:S(2)}) async-start(), calls=%async_computation.31 | async-start | bytes 1179648 | tf_op jit(solution)/shard_map/reduce_scatter | solution.py:190
  623.6 291.2 %all-reduce.5.cloned.1.call-start = ((), (), s32[]{:S(2)}) async-start(), calls=%async_computation.32 | async-start | bytes 28311552 | tf_op jit(solution)/shard_map/psum | solution.py:197
  632.0 71.0 %copy-start.105 = (bf16[1,256,768]{2,1,0:T(8,128)(2,1)S(1)}, bf16[1,256,768]{2,1,0:T(8,128)(2,1)}, u32[]{:S(2)}) copy-start(bf16[1,256,768]{2,1,0:T(8,128)(2,1)} %get-tuple-element.114) | copy-start | bytes 1179652
  632.0 71.0 %copy-start.112 = (bf16[1,256,768]{2,1,0:T(8,128)(2,1)S(1)}, bf16[1,256,768]{2,1,0:T(8,128)(2,1)}, u32[]{:S(2)}) copy-start(bf16[1,256,768]{2,1,0:T(8,128)(2,1)} %get-tuple-element.117) | copy-start | bytes 1179652
  632.0 71.0 %copy-start.116 = (bf16[1,256,768]{2,1,0:T(8,128)(2,1)S(1)}, bf16[1,256,768]{2,1,0:T(8,128)(2,1)}, u32[]{:S(2)}) copy-start(bf16[1,256,768]{2,1,0:T(8,128)(2,1)} %get-tuple-element.115) | copy-start | bytes 1179652
  632.0 75.2 %copy-start.141 = (f32[768]{0:T(1024)S(1)}, f32[768]{0:T(1024)}, u32[]{:S(2)}) copy-start(f32[768]{0:T(1024)} %param.21) | copy-start | bytes 9220
  632.0 75.2 %copy-start.145 = (f32[256]{0:T(256)S(1)}, f32[256]{0:T(256)}, u32[]{:S(2)}) copy-start(f32[256]{0:T(256)} %copy-done.144) | copy-start | bytes 3076
  707.2 52.6 %copy-start.44 = (f32[1,256,768]{2,1,0:T(8,128)S(1)}, f32[1,256,768]{2,1,0:T(8,128)}, u32[]{:S(2)}) copy-start(f32[1,256,768]{2,1,0:T(8,128)} %copy-done.43) | copy-start | bytes 2359300
  707.2 52.7 %copy-start.150 = (f32[256]{0:T(256)S(1)}, f32[256]{0:T(256)}, u32[]{:S(2)}) copy-start(f32[256]{0:T(256)} %copy-done.149) | copy-start | bytes 3076
  707.2 52.6 %copy-start.117 = (bf16[1,256,768]{2,1,0:T(8,128)(2,1)S(1)}, bf16[1,256,768]{2,1,0:T(8,128)(2,1)}, u32[]{:S(2)}) copy-start(bf16[1,256,768]{2,1,0:T(8,128)(2,1)} %reduce-scatter.47.cloned.1.call-done) | copy-start | bytes 1179652
  (191 other events, 1234.1 us)
Sparse Core Ops, SparseCore 0:
  38.1 31.3 reduce-scatter.24
  101.3 27.2 reduce-scatter.40
  131.3 17.4 reduce-scatter.26
  179.4 17.4 reduce-scatter.42
  227.4 29.7 reduce-scatter.28
  260.0 29.1 reduce-scatter.20
  292.0 37.1 reduce-scatter.16
  382.2 26.8 reduce-scatter.36
  411.4 26.0 reduce-scatter.44
  439.7 26.0 reduce-scatter.32
  468.6 17.4 reduce-scatter.18
  488.8 17.4 reduce-scatter.30
  509.1 23.6 reduce-scatter.22
  588.8 17.3 reduce-scatter.34
  609.3 17.3 reduce-scatter.38
  629.5 17.4 reduce-scatter.46
  653.1 261.7 all-reduce.4
where the time goes:
time: 940 us; the launch traced here: 932 us
  blocking collectives  307 us (33%)
  waiting for transfers between devices  255 us (27%)
  matrix products  229 us (24%)
  other arithmetic  87.3 us (9%)
  local copies, waits for them, and re-layouts  37.1 us (4%)
  between operations  16.6 us (2%)
    dot_general x96, matrix products, product(): jnp.einsum(pattern, left_side, right_side, preferred_element_type=jnp.flo...  229 us
    psum x1, waiting for transfers between devices, on_device(): lax.psum((sum_w_query, sum_b_query, sum_w_key, sum_w_value, sum_b_value,...  152 us
    all_gather x4, blocking collectives, on_device(): grad_full = lax.all_gather(upstream, 'mp', axis=1, tiled=True)  61.7 us
    psum x1, blocking collectives, on_device(): lax.psum((sum_w_query, sum_b_query, sum_w_key, sum_w_value, sum_b_value,...  60.4 us
    all_gather x4, blocking collectives, on_device(): lax.all_gather(normed_in.astype(jnp.bfloat16), 'mp', axis=1, tiled=True)  51.1 us
    reduce_scatter x4, waiting for transfers between devices, on_device(): lax.psum_scatter(product('bsf,fd->bsd', active, w_down).astype(jnp.bfloat...  51 us
    all_gather x4, blocking collectives, on_device(): lax.all_gather(grad_residual.astype(jnp.bfloat16), 'mp', axis=1, tiled=True)  48.7 us
    all_gather x4, blocking collectives, on_device(): lax.all_gather(normed_mid.astype(jnp.bfloat16), 'mp', axis=1, tiled=True)  45.3 us
  transfers between devices with their start and end apart: 17, of which 8 were waited for; matrix products, arithmetic and copies ran while one was open for 23% of the time, Pallas kernels for 0%

commit v1 on v0

--- a/solution.py
+++ b/solution.py
@@ -10,6 +10,18 @@
 ROWS_MB = 1
 epsilon = 1e-12
 masked_fill = -1000000000.0
+
+
+def doubled_up(value, axis, dim):
+    ways, here, lap = (lax.axis_size(axis), lax.axis_index(axis), value.shape[dim])
+    line, have = (value, 1)
+    while have < ways:
+        line = jnp.concatenate(
+            [line, lax.ppermute(line, axis, [(d, (d - have) % ways) for d in range(ways)])],
+            axis=dim,
+        )
+        have = 2 * have
+    return jnp.roll(line, here * lap, axis=dim)
 
 
 def layer_norm(values, gain_vec, offset):
@@ -93,7 +105,7 @@
         row_lengths = lengths[row_start : row_start + ROWS_MB]
         upstream = out_grad[row_start : row_start + ROWS_MB]
         normed_in, unit_in, inv_in = layer_norm(inputs, ln1_gain, ln1_shift)
-        full_in = lax.all_gather(normed_in.astype(jnp.bfloat16), "mp", axis=1, tiled=True)
+        full_in = doubled_up(normed_in.astype(jnp.bfloat16), "mp", 1)
         rows_mb = full_in.shape[0]
         query_low = (
             (product("bsd,de->bse", full_in, w_query) + b_query)

time: 940 us -> 940 us (level)
  blocking collectives: 307 us -> 256 us
  waiting for transfers between devices: 255 us -> 291 us
    all_gather x4 -> x0, blocking collectives: 51.1 us -> none  [on_device(): lax.all_gather(normed_in.astype(jnp.bfloat16), 'mp', axis=1, tiled=True)]
    reduce_scatter x4, waiting for transfers between devices: 13 us -> 31.7 us  [on_device(): lax.psum_scatter(product('bse,ed->bsd', mixed_low, w_out), 'mp', scatter_...]
    ppermute x0 -> x4, waiting for transfers between devices: none -> 16.6 us  [doubled_up(): lax.ppermute(line, axis, [(d, (d - have) % ways) for d in range(ways)])]
    unnamed x418 -> x434, local copies, waits for them, and re-layouts: 31.2 us -> 30.2 us
  transfers between devices with their start and end apart: 17 -> 21, of which waited for: 8 -> 10; matrix products, arithmetic and copies ran while one was open for 23% -> 24% of each run, Pallas kernels for 0% -> 0%
where the time goes in v1:
time: 940 us; the launch traced here: 932 us
  waiting for transfers between devices  291 us (31%)
  blocking collectives  256 us (27%)
  matrix products  228 us (24%)
  other arithmetic  96 us (10%)
  local copies, waits for them, and re-layouts  36.7 us (4%)
  between operations  16.8 us (2%)
    dot_general x96, matrix products, product(): jnp.einsum(pattern, left_side, right_side, preferred_element_type=jnp.flo...  228 us
    psum x1, waiting for transfers between devices, on_device(): lax.psum((sum_w_query, sum_b_query, sum_w_key, sum_w_value, sum_b_value,...  153 us
    all_gather x4, blocking collectives, on_device(): grad_full = lax.all_gather(upstream, 'mp', axis=1, tiled=True)  63.8 us
    psum x1, blocking collectives, on_device(): lax.psum((sum_w_query, sum_b_query, sum_w_key, sum_w_value, sum_b_value,...  60.3 us
    reduce_scatter x4, waiting for transfers between devices, on_device(): lax.psum_scatter(product('bsf,fd->bsd', active, w_down).astype(jnp.bfloat...  49.8 us
    all_gather x4, blocking collectives, on_device(): lax.all_gather(grad_residual.astype(jnp.bfloat16), 'mp', axis=1, tiled=True)  48.4 us
    all_gather x4, blocking collectives, on_device(): lax.all_gather(normed_mid.astype(jnp.bfloat16), 'mp', axis=1, tiled=True)  44.2 us
    psum x1, blocking collectives, on_device(): lax.psum((sum_ln1_gain, sum_ln1_shift, sum_ln2_gain, sum_ln2_shift, sum_b...  39.3 us
  transfers between devices with their start and end apart: 21, of which 10 were waited for; matrix products, arithmetic and copies ran while one was open for 24% of the time, Pallas kernels for 0%

profile of v1, /device:TPU:0, one launch (start us, length us, event | category | flops | bytes accessed | tf_op | source)
XLA Modules:
  0.0 931.9 jit_solution(13502382230643735918)
XLA Ops:
  18.0 7.3 collective-permute-done.2
  41.4 16.8 %all_gather.44 = bf16[1,512,768]{2,1,0:T(8,128)(2,1)} all-gather(bf16[1,256,768]{2,1,0:T(8,128)(2,1)S(1)} %get-tuple-element.114), channel_id=1, replica_groups=mesh['dp'=16,'mp'=2] {'mp'}, dimensions={1}, use_global_device_ids=true | all-gather | bytes 1179648 | tf_op jit(solution)/shard_map/all_gather | solution.py:150
  58.2 12.3 %reduce-scatter.25.cloned.1.call-done = f32[1,256,768]{2,1,0:T(8,128)} async-done(((f32[1,512,768]{2,1,0:T(8,128)}), f32[1,256,768]{2,1,0:T(8,128)}) %reduce-scatter.25.cloned.1.call-update) | async-done | bytes 786448 | tf_op jit(solution)/shard_map/reduce_scatter | solution.py:135
  73.1 11.9 %all_gather.38 = bf16[1,512,768]{2,1,0:T(8,128)(2,1)S(1)} all-gather(bf16[1,256,768]{2,1,0:T(8,128)(2,1)S(1)} %add_convert_fusion.7), channel_id=1, replica_groups=mesh['dp'=16,'mp'=2] {'mp'}, dimensions={1}, use_global_device_ids=true | all-gather | bytes 1179648 | tf_op jit(solution)/shard_map/all_gather | solution.py:140
  85.1 10.3 %fusion.16 = (bf16[512,1536]{1,0:T(8,128)(2,1)}, f32[512,1536]{1,0:T(8,128)S(1)}) fusion(f32[1536]{0:T(1024)} %param.35, bf16[768,1536]{1,0:T(8,128)(2,1)S(1)} %copy-done, bf16[1,512,768]{2,1,0:T(8,128)(2,1)S(1)} %all_gather.38), kind=kOutput, calls=%fused_computation.54 | convolution fusion | flops 1259864064 | bytes 7870464 | tf_op jit(solution)/shard_map/bsd,df->bsf/dot_general | solution.py:50
  106.4 22.8 %reduce-scatter.41.cloned.1.call-done = f32[1,256,768]{2,1,0:T(8,128)} async-done(((f32[1,512,768]{2,1,0:T(8,128)}), f32[1,256,768]{2,1,0:T(8,128)}) %reduce-scatter.41.cloned.1.call-update) | async-done | bytes 786448 | tf_op jit(solution)/shard_map/reduce_scatter | solution.py:159
  132.0 17.6 %reduce-scatter.27.cloned.1.call-done = bf16[1,256,768]{2,1,0:T(8,128)(2,1)} async-done(((bf16[1,512,768]{2,1,0:T(8,128)(2,1)}), bf16[1,256,768]{2,1,0:T(8,128)(2,1)}) %reduce-scatter.27.cloned.1.call-update) | async-done | bytes 393232 | tf_op jit(solution)/shard_map/reduce_scatter | solution.py:143
  153.2 11.5 %all_gather.45 = bf16[1,512,768]{2,1,0:T(8,128)(2,1)S(1)} all-gather(bf16[1,256,768]{2,1,0:T(8,128)(2,1)S(1)} %convert_element_type.620), channel_id=1, replica_groups=mesh['dp'=16,'mp'=2] {'mp'}, dimensions={1}, use_global_device_ids=true | all-gather | bytes 1179648 | tf_op jit(solution)/shard_map/all_gather | solution.py:166
  180.5 16.6 %reduce-scatter.43.cloned.1.call-done = bf16[1,256,768]{2,1,0:T(8,128)(2,1)} async-done(((bf16[1,512,768]{2,1,0:T(8,128)(2,1)}), bf16[1,256,768]{2,1,0:T(8,128)(2,1)}) %reduce-scatter.43.cloned.1.call-update) | async-done | bytes 393232 | tf_op jit(solution)/shard_map/reduce_scatter | solution.py:202
  205.5 9.3 collective-permute-done.3
  262.0 20.3 %all_gather.46 = bf16[1,512,768]{2,1,0:T(8,128)(2,1)} all-gather(bf16[1,256,768]{2,1,0:T(8,128)(2,1)} %get-tuple-element.113), channel_id=1, replica_groups=mesh['dp'=16,'mp'=2] {'mp'}, dimensions={1}, use_global_device_ids=true | all-gather | bytes 1179648 | tf_op jit(solution)/shard_map/all_gather | solution.py:150
  282.3 18.2 %all_gather.42 = bf16[1,512,768]{2,1,0:T(8,128)(2,1)} all-gather(bf16[1,256,768]{2,1,0:T(8,128)(2,1)} %get-tuple-element.112), channel_id=1, replica_groups=mesh['dp'=16,'mp'=2] {'mp'}, dimensions={1}, use_global_device_ids=true | all-gather | bytes 1179648 | tf_op jit(solution)/shard_map/all_gather | solution.py:150
  300.5 8.5 all_gather.40
  309.1 19.4 %reduce-scatter.17.cloned.1.call-done = f32[1,256,768]{2,1,0:T(8,128)} async-done(((f32[1,512,768]{2,1,0:T(8,128)}), f32[1,256,768]{2,1,0:T(8,128)}) %reduce-scatter.17.cloned.1.call-update) | async-done | bytes 786448 | tf_op jit(solution)/shard_map/reduce_scatter | solution.py:135
  332.1 11.6 %all_gather.39 = bf16[1,512,768]{2,1,0:T(8,128)(2,1)} all-gather(bf16[1,256,768]{2,1,0:T(8,128)(2,1)S(1)} %get-tuple-element.121), channel_id=1, replica_groups=mesh['dp'=16,'mp'=2] {'mp'}, dimensions={1}, use_global_device_ids=true | all-gather | bytes 1179648 | tf_op jit(solution)/shard_map/all_gather | solution.py:140
  343.7 10.6 %all_gather.37 = bf16[1,512,768]{2,1,0:T(8,128)(2,1)S(1)} all-gather(bf16[1,256,768]{2,1,0:T(8,128)(2,1)S(1)} %get-tuple-element.120), channel_id=1, replica_groups=mesh['dp'=16,'mp'=2] {'mp'}, dimensions={1}, use_global_device_ids=true | all-gather | bytes 1179648 | tf_op jit(solution)/shard_map/all_gather | solution.py:140
  354.4 9.4 %fusion.13 = (bf16[512,1536]{1,0:T(8,128)(2,1)}, f32[512,1536]{1,0:T(8,128)S(1)}) fusion(f32[1536]{0:T(1024)S(1)} %copy-done.192, bf16[768,1536]{1,0:T(8,128)(2,1)S(1)} %copy-done, bf16[1,512,768]{2,1,0:T(8,128)(2,1)S(1)} %all_gather.37), kind=kOutput, calls=%fused_computation.51 | convolution fusion | flops 1259864064 | bytes 7870464 | tf_op jit(solution)/shard_map/bsd,df->bsf/dot_general | solution.py:50
  363.8 10.0 %all_gather.36 = bf16[1,512,768]{2,1,0:T(8,128)(2,1)} all-gather(bf16[1,256,768]{2,1,0:T(8,128)(2,1)S(1)} %get-tuple-element.119), channel_id=1, replica_groups=mesh['dp'=16,'mp'=2] {'mp'}, dimensions={1}, use_global_device_ids=true | all-gather | bytes 1179648 | tf_op jit(solution)/shard_map/all_gather | solution.py:140
  380.6 9.8 %fusion.19 = (bf16[512,1536]{1,0:T(8,128)(2,1)}, f32[512,1536]{1,0:T(8,128)S(1)}) fusion(f32[1536]{0:T(1024)S(1)} %copy-done.192, bf16[768,1536]{1,0:T(8,128)(2,1)S(1)} %copy-done, bf16[1,512,768]{2,1,0:T(8,128)(2,1)} %all_gather.39), kind=kOutput, calls=%fused_computation.57 | convolution fusion | flops 1259864064 | bytes 7870464 | tf_op jit(solution)/shard_map/bsd,df->bsf/dot_general | solution.py:50
  397.5 9.8 %fusion.10 = (bf16[512,1536]{1,0:T(8,128)(2,1)}, f32[512,1536]{1,0:T(8,128)S(1)}) fusion(f32[1536]{0:T(1024)S(1)} %copy-done.192, bf16[768,1536]{1,0:T(8,128)(2,1)S(1)} %copy-done, bf16[1,512,768]{2,1,0:T(8,128)(2,1)} %all_gather.36), kind=kOutput, calls=%fused_computation.48 | convolution fusion | flops 1259864064 | bytes 7870464 | tf_op jit(solution)/shard_map/bsd,df->bsf/dot_general | solution.py:50
  419.0 5.4 fusion.178
  434.1 5.5 fusion.197
  449.1 9.7 %add_add_fusion = f32[1536,768]{1,0:T(8,128)} fusion(f32[1536,768]{1,0:T(8,128)} %fusion.178, f32[1536,768]{1,0:T(8,128)} %fusion.189, f32[1536,768]{1,0:T(8,128)} %fusion.183, bf16[512,1536]{1,0:T(8,128)(2,1)} %get-tuple-element.146, bf16[1,512,768]{2,1,0:T(8,128)(2,1)} %all_gather.46), kind=kOutput, calls=%fused_computation.32 | convolution fusion | flops 1211498496 | bytes 21233664 | tf_op jit(solution)/shard_map/bsf,bsd->fd/dot_general | solution.py:50
  458.8 9.1 add_add_fusion.1
  471.7 12.0 %reduce-scatter.19.cloned.1.call-done = bf16[1,256,768]{2,1,0:T(8,128)(2,1)} async-done(((bf16[1,512,768]{2,1,0:T(8,128)(2,1)}), bf16[1,256,768]{2,1,0:T(8,128)(2,1)}) %reduce-scatter.19.cloned.1.call-update) | async-done | bytes 393232 | tf_op jit(solution)/shard_map/reduce_scatter | solution.py:143
  483.7 20.2 %reduce-scatter.31.cloned.1.call-done = bf16[1,256,768]{2,1,0:T(8,128)(2,1)} async-done(((bf16[1,512,768]{2,1,0:T(8,128)(2,1)}), bf16[1,256,768]{2,1,0:T(8,128)(2,1)}) %reduce-scatter.31.cloned.1.call-update) | async-done | bytes 393232 | tf_op jit(solution)/shard_map/reduce_scatter | solution.py:143
  509.5 19.6 %all_gather.41 = bf16[1,512,768]{2,1,0:T(8,128)(2,1)S(1)} all-gather(bf16[1,256,768]{2,1,0:T(8,128)(2,1)S(1)} %convert_element_type.586), channel_id=1, replica_groups=mesh['dp'=16,'mp'=2] {'mp'}, dimensions={1}, use_global_device_ids=true | all-gather | bytes 1179648 | tf_op jit(solution)/shard_map/all_gather | solution.py:166
  540.1 8.5 all_gather.43
  568.5 8.9 all_gather.47
  641.2 60.3 %all-reduce.1 = (f32[384]{0:T(512)}, f32[384]{0:T(512)}, f32[1536]{0:T(1024)}) all-reduce(f32[384]{0:T(512)} %add.708, f32[384]{0:T(512)} %add.718, f32[1536]{0:T(1024)S(1)} %add_add_fusion.2), channel_id=1, replica_groups=mesh['dp'=16,'mp'=2] {'dp'}, use_global_device_ids=true, to_apply=%region_75.77 | all-reduce | flops 2304 | bytes 18432 | tf_op jit(solution)/shard_map/psum | solution.py:209
  712.2 39.3 %all-reduce = (f32[768]{0:T(1024)}, f32[768]{0:T(1024)}, f32[768]{0:T(1024)}, f32[768]{0:T(1024)}, f32[768]{0:T(1024)}, /*index=5*/f32[768]{0:T(1024)}) all-reduce(f32[768]{0:T(1024)} %add_add_fusion.10, f32[768]{0:T(1024)} %add_add_fusion.9, f32[768]{0:T(1024)} %add_add_fusion.6, ...), channel_id=1, replica_groups=mesh['dp'=16,'mp'=2] {'dp','mp'}, use_global_device_ids=true, to_apply=%region_64.66 | all-reduce | flops 4608 | bytes 36864 | tf_op jit(solution)/shard_map/psum | solution.py:224
  761.7 152.7 %all-reduce.5.cloned.1.call-done = (f32[768,384]{1,0:T(8,128)}, f32[768,384]{1,0:T(8,128)}, f32[768,384]{1,0:T(8,128)}, f32[384,768]{1,0:T(8,128)}, f32[768,1536]{1,0:T(8,128)}, /*index=5*/f32[1536,768]{1,0:T(8,128)}) async-done(((f32[768,384]{1,0:T(8,128)}, f32[768,384]{1,0:T(8,128)}, f32[768,384]{1,0:T(8,128)}, f32[384,768]{1,0:T(8,128)}, f32[768,1536]{1,0:T(8,128)}, /*index=5*/f32[1536,768]{1,0:T(8,128)}), ...) | async-done | bytes 14155792 | tf_op jit(solution)/shard_map/psum | solution.py:209
  (672 shorter events, 299.8 us)
Async XLA Ops:
  7.2 77.9 %copy-start = (bf16[768,1536]{1,0:T(8,128)(2,1)S(1)}, bf16[768,1536]{1,0:T(8,128)(2,1)}, u32[]{:S(2)}) copy-start(bf16[768,1536]{1,0:T(8,128)(2,1)} %param.34) | copy-start | bytes 7077892
  7.2 63.3 %reduce-scatter.25.cloned.1.call-start = ((), (), s32[]{:S(2)}) async-start(), calls=%async_computation.20 | async-start | bytes 2359296 | tf_op jit(solution)/shard_map/reduce_scatter | solution.py:135
  12.9 12.4 %collective-permute-start.2 = (bf16[1,256,768]{2,1,0:T(8,128)(2,1)}, bf16[1,256,768]{2,1,0:T(8,128)(2,1)}, u32[]{:S(2)}, u32[]{:S(2)}) collective-permute-start(bf16[1,256,768]{2,1,0:T(8,128)(2,1)} %fusion.127), channel_id=1, source_target_pairs={{0,1},{1,0},{2,3},{3,2},{4,5},{5,4},{6,7},{7,6},{8,9},{9,8},{10,11... | collective-permute-start | bytes 1179656 | tf_op jit(solution)/shard_map/ppermute | solution.py:20
  39.0 90.3 %reduce-scatter.41.cloned.1.call-start = ((), (), s32[]{:S(2)}) async-start(), calls=%async_computation.28 | async-start | bytes 2359296 | tf_op jit(solution)/shard_map/reduce_scatter | solution.py:159
  101.9 47.7 %reduce-scatter.27.cloned.1.call-start = ((), (), s32[]{:S(2)}) async-start(), calls=%async_computation.21 | async-start | bytes 1179648 | tf_op jit(solution)/shard_map/reduce_scatter | solution.py:143
  106.4 90.8 %reduce-scatter.43.cloned.1.call-start = ((), (), s32[]{:S(2)}) async-start(), calls=%async_computation.29 | async-start | bytes 1179648 | tf_op jit(solution)/shard_map/reduce_scatter | solution.py:202
  179.6 129.5 %reduce-scatter.29.cloned.1.call-start = ((), (), s32[]{:S(2)}) async-start(), calls=%async_computation.22 | async-start | bytes 2359296 | tf_op jit(solution)/shard_map/reduce_scatter | solution.py:135
  202.8 12.0 %collective-permute-start.3 = (bf16[1,256,768]{2,1,0:T(8,128)(2,1)S(1)}, bf16[1,256,768]{2,1,0:T(8,128)(2,1)S(1)}, u32[]{:S(2)}, u32[]{:S(2)}) collective-permute-start(bf16[1,256,768]{2,1,0:T(8,128)(2,1)S(1)} %get-tuple-element.98), channel_id=1, source_target_pairs={{0,1},{1,0},{2,3},{3,2},{4,5},{5,4},{6,7},{7,6},{8,9},{9,8},{10,11... | collective-permute-start | bytes 1179656 | tf_op jit(solution)/shard_map/ppermute | solution.py:20
  203.7 27.4 %collective-permute-start.1 = (bf16[1,256,768]{2,1,0:T(8,128)(2,1)}, bf16[1,256,768]{2,1,0:T(8,128)(2,1)}, u32[]{:S(2)}, u32[]{:S(2)}) collective-permute-start(bf16[1,256,768]{2,1,0:T(8,128)(2,1)} %get-tuple-element.97), channel_id=1, source_target_pairs={{0,1},{1,0},{2,3},{3,2},{4,5},{5,4},{6,7},{7,6},{8,9},{9,8},{10,11... | collective-permute-start | bytes 1179656 | tf_op jit(solution)/shard_map/ppermute | solution.py:20
  229.6 79.5 %reduce-scatter.21.cloned.1.call-start = ((), (), s32[]{:S(2)}) async-start(), calls=%async_computation.18 | async-start | bytes 2359296 | tf_op jit(solution)/shard_map/reduce_scatter | solution.py:135
  230.7 16.3 %collective-permute-start = (bf16[1,256,768]{2,1,0:T(8,128)(2,1)}, bf16[1,256,768]{2,1,0:T(8,128)(2,1)}, u32[]{:S(2)}, u32[]{:S(2)}) collective-permute-start(bf16[1,256,768]{2,1,0:T(8,128)(2,1)} %get-tuple-element.96), channel_id=1, source_target_pairs={{0,1},{1,0},{2,3},{3,2},{4,5},{5,4},{6,7},{7,6},{8,9},{9,8},{10,11... | collective-permute-start | bytes 1179656 | tf_op jit(solution)/shard_map/ppermute | solution.py:20
  246.1 82.4 %reduce-scatter.17.cloned.1.call-start = ((), (), s32[]{:S(2)}) async-start(), calls=%async_computation.16 | async-start | bytes 2359296 | tf_op jit(solution)/shard_map/reduce_scatter | solution.py:135
  261.9 66.5 %copy-start.169 = (f32[768]{0:T(1024)S(1)}, f32[768]{0:T(1024)}, u32[]{:S(2)}) copy-start(f32[768]{0:T(1024)} %param.31) | copy-start | bytes 9220
  262.0 206.0 %reduce-scatter.37.cloned.1.call-start = ((), (), s32[]{:S(2)}) async-start(), calls=%async_computation.26 | async-start | bytes 2359296 | tf_op jit(solution)/shard_map/reduce_scatter | solution.py:159
  331.1 136.9 %copy-start.149 = (f32[256]{0:T(256)}, f32[256]{0:T(256)S(1)}, u32[]{:S(2)}) copy-start(f32[256]{0:T(256)S(1)} %broadcast_multiply_fusion.20) | copy-start | bytes 3076
  331.3 136.6 %copy-start.175 = (f32[256]{0:T(256)}, f32[256]{0:T(256)S(1)}, u32[]{:S(2)}) copy-start(f32[256]{0:T(256)S(1)} %add_rsqrt_fusion.4) | copy-start | bytes 3076
  380.5 87.4 %reduce-scatter.45.cloned.1.call-start = ((), (), s32[]{:S(2)}) async-start(), calls=%async_computation.30 | async-start | bytes 2359296 | tf_op jit(solution)/shard_map/reduce_scatter | solution.py:159
  397.0 70.9 %reduce-scatter.33.cloned.1.call-start = ((), (), s32[]{:S(2)}) async-start(), calls=%async_computation.24 | async-start | bytes 2359296 | tf_op jit(solution)/shard_map/reduce_scatter | solution.py:159
  413.9 69.8 %reduce-scatter.19.cloned.1.call-start = ((), (), s32[]{:S(2)}) async-start(), calls=%async_computation.17 | async-start | bytes 1179648 | tf_op jit(solution)/shard_map/reduce_scatter | solution.py:143
  418.9 85.0 %reduce-scatter.31.cloned.1.call-start = ((), (), s32[]{:S(2)}) async-start(), calls=%async_computation.23 | async-start | bytes 1179648 | tf_op jit(solution)/shard_map/reduce_scatter | solution.py:143
  433.8 103.0 %reduce-scatter.23.cloned.1.call-start = ((), (), s32[]{:S(2)}) async-start(), calls=%async_computation.19 | async-start | bytes 1179648 | tf_op jit(solution)/shard_map/reduce_scatter | solution.py:143
  449.0 256.8 %reduce-scatter.35.cloned.1.call-start = ((), (), s32[]{:S(2)}) async-start(), calls=%async_computation.25 | async-start | bytes 1179648 | tf_op jit(solution)/shard_map/reduce_scatter | solution.py:202
  589.0 116.8 %reduce-scatter.39.cloned.1.call-start = ((), (), s32[]{:S(2)}) async-start(), calls=%async_computation.27 | async-start | bytes 1179648 | tf_op jit(solution)/shard_map/reduce_scatter | solution.py:202
  607.8 98.0 %reduce-scatter.47.cloned.1.call-start = ((), (), s32[]{:S(2)}) async-start(), calls=%async_computation.31 | async-start | bytes 1179648 | tf_op jit(solution)/shard_map/reduce_scatter | solution.py:202
  622.3 292.1 %all-reduce.5.cloned.1.call-start = ((), (), s32[]{:S(2)}) async-start(), calls=%async_computation.32 | async-start | bytes 28311552 | tf_op jit(solution)/shard_map/psum | solution.py:209
  630.6 70.9 %copy-start.108 = (bf16[1,256,768]{2,1,0:T(8,128)(2,1)S(1)}, bf16[1,256,768]{2,1,0:T(8,128)(2,1)}, u32[]{:S(2)}) copy-start(bf16[1,256,768]{2,1,0:T(8,128)(2,1)} %get-tuple-element.115) | copy-start | bytes 1179652
  630.6 70.9 %copy-start.115 = (bf16[1,256,768]{2,1,0:T(8,128)(2,1)S(1)}, bf16[1,256,768]{2,1,0:T(8,128)(2,1)}, u32[]{:S(2)}) copy-start(bf16[1,256,768]{2,1,0:T(8,128)(2,1)} %get-tuple-element.118) | copy-start | bytes 1179652
  630.6 70.9 %copy-start.119 = (bf16[1,256,768]{2,1,0:T(8,128)(2,1)S(1)}, bf16[1,256,768]{2,1,0:T(8,128)(2,1)}, u32[]{:S(2)}) copy-start(bf16[1,256,768]{2,1,0:T(8,128)(2,1)} %get-tuple-element.116) | copy-start | bytes 1179652
  630.6 75.2 %copy-start.143 = (f32[768]{0:T(1024)S(1)}, f32[768]{0:T(1024)}, u32[]{:S(2)}) copy-start(f32[768]{0:T(1024)} %param.23) | copy-start | bytes 9220
  630.6 75.2 %copy-start.148 = (f32[256]{0:T(256)S(1)}, f32[256]{0:T(256)}, u32[]{:S(2)}) copy-start(f32[256]{0:T(256)} %copy-done.147) | copy-start | bytes 3076
  705.8 52.6 %copy-start.46 = (f32[1,256,768]{2,1,0:T(8,128)S(1)}, f32[1,256,768]{2,1,0:T(8,128)}, u32[]{:S(2)}) copy-start(f32[1,256,768]{2,1,0:T(8,128)} %copy-done.45) | copy-start | bytes 2359300
  705.8 52.6 %copy-start.153 = (f32[256]{0:T(256)S(1)}, f32[256]{0:T(256)}, u32[]{:S(2)}) copy-start(f32[256]{0:T(256)} %copy-done.152) | copy-start | bytes 3076
  (203 other events, 1416.7 us)
Sparse Core Ops, SparseCore 0:
  39.1 31.3 reduce-scatter.24
  102.0 27.2 reduce-scatter.40
  132.1 17.4 reduce-scatter.26
  179.7 17.4 reduce-scatter.42
  229.7 28.2 reduce-scatter.28
  260.7 38.1 reduce-scatter.20
  301.7 26.6 reduce-scatter.16
  380.6 26.0 reduce-scatter.36
  409.0 26.0 reduce-scatter.44
  437.3 26.0 reduce-scatter.32
  466.2 17.4 reduce-scatter.18
  486.5 17.4 reduce-scatter.30
  506.7 24.0 reduce-scatter.22
  589.1 17.4 reduce-scatter.34
  608.7 17.4 reduce-scatter.38
  629.0 17.4 reduce-scatter.46
  652.6 261.7 all-reduce.4
